TPU v7x, 32 devices: a whole 2x2x4 slice. The times are simulated.
32 devices in a mesh: dp: 16 (over z, y, core), mp: 2 (over x).
Axes of the slice: x: 2, y: 2, z: 4, core: 2. Of those that a mesh axis runs over, the one named last changes fastest.
Arguments:
- hidden_in: bfloat16 [32768, 1024], P(('dp', 'mp')), may hold values from -6 to 6
- out_grad: bfloat16 [32768, 1024], P(('dp', 'mp')), may hold values from -6 to 6
- ln1_gain: float32 [1024], replicated, may hold values from 0.5 to 1.5
- ln1_bias: float32 [1024], replicated, may hold values from -3 to 3
- w_query: bfloat16 [1024, 1024], P(None, 'mp'), may hold values from -0.1875 to 0.1875
- w_key: bfloat16 [1024, 1024], P(None, 'mp'), may hold values from -0.1875 to 0.1875
- w_value: bfloat16 [1024, 1024], P(None, 'mp'), may hold values from -0.1875 to 0.1875
- w_out: bfloat16 [1024, 1024], P('mp'), may hold values from -1.5 to 1.5
- ln2_gain: float32 [1024], replicated, may hold values from 0.5 to 1.5
- ln2_bias: float32 [1024], replicated, may hold values from -3 to 3
- w_up: bfloat16 [1024, 4096], P(None, 'mp'), may hold values from -0.1875 to 0.1875
- b_up: float32 [4096], P('mp'), may hold values from -3 to 3
- w_down: bfloat16 [4096, 1024], P('mp'), may hold values from -0.09375 to 0.09375
- b_down: float32 [1024], replicated, may hold values from -3 to 3
- rand_blocks: int32 [16, 16, 3], P('mp'), may hold values from 0 to 15
Outputs:
- output: bfloat16 [32768, 1024], P(('dp', 'mp'))
- input_grad: float32 [32768, 1024], P(('dp', 'mp'))
- grad_ln1_gain: float32 [1024], replicated
- grad_ln1_bias: float32 [1024], replicated
- grad_w_query: float32 [1024, 1024], P(None, 'mp')
- grad_w_key: float32 [1024, 1024], P(None, 'mp')
- grad_w_value: float32 [1024, 1024], P(None, 'mp')
- grad_w_out: float32 [1024, 1024], P('mp')
- grad_ln2_gain: float32 [1024], replicated
- grad_ln2_bias: float32 [1024], replicated
- grad_w_up: float32 [1024, 4096], P(None, 'mp')
- grad_b_up: float32 [4096], P('mp')
- grad_w_down: float32 [4096, 1024], P('mp')
- grad_b_down: float32 [1024], replicated
Inputs may be any that keep to these rules, and one draw needn't show every extreme that they name: rand_blocks[h, i, r] is a key block of the same sequence; entries may repeat or fall on window or global blocks, and those of the first and last query blocks have no effect.
All inputs are finite; a program needn't handle non-finite values.
Results may differ from a plain program's by a relative error of at most 0.02.
Values may be sent and summed in bfloat16 or wider, within the bound.
A program may use at most 320 MiB of HBM per device.

v0:
```python
import jax
import jax.numpy as jnp
from jax import lax
from jax.sharding import PartitionSpec as P

HD = 64
BLOCK = 64
SEQ = 1024


def layer_norm(values, norm_gain, norm_bias):
    center = values - jnp.mean(values, axis=-1, keepdims=True)
    spread = jnp.mean(center * center, axis=-1, keepdims=True)
    return center * lax.rsqrt(spread + 1e-05) * norm_gain + norm_bias


def block_mask(rand_blocks):
    blocks = SEQ // BLOCK
    row_ids = jnp.arange(blocks)[:, None]
    col_ids = jnp.arange(blocks)[None, :]
    window = (
        (jnp.abs(row_ids - col_ids) <= 1)
        | (col_ids == 0)
        | (col_ids == blocks - 1)
        | (row_ids == 0)
        | (row_ids == blocks - 1)
    )
    picked = jnp.any(rand_blocks[:, :, :, None] == jnp.arange(blocks)[None, None, None, :], axis=2)
    allowed = window[None] | picked
    return jnp.repeat(jnp.repeat(allowed, BLOCK, axis=1), BLOCK, axis=2)


def attend_forward(joined_seq, allowed, scaling):
    queries = joined_seq[:, 0]
    key_rows = joined_seq[:, 1]
    value_rows = joined_seq[:, 2]
    scores = (
        jnp.einsum("qhd,khd->hqk", queries, key_rows, preferred_element_type=jnp.float32) * scaling
    )
    scores = jnp.where(allowed, scores, -1e30)
    highest = jnp.max(scores, axis=-1, keepdims=True)
    shifted = jnp.exp(scores - highest)
    row_totals = jnp.sum(shifted, axis=-1, keepdims=True)
    attn_probs = (shifted / row_totals).astype(jnp.bfloat16)
    context = jnp.einsum("hqk,khd->qhd", attn_probs, value_rows, preferred_element_type=jnp.float32)
    return (context.astype(jnp.bfloat16), (highest + jnp.log(row_totals))[..., 0])


def attend_backward(seq_items, allowed, scaling):
    joined_seq, grad_context, row_lse = seq_items
    queries = joined_seq[:, 0]
    key_rows = joined_seq[:, 1]
    value_rows = joined_seq[:, 2]
    scores = (
        jnp.einsum("qhd,khd->hqk", queries, key_rows, preferred_element_type=jnp.float32) * scaling
    )
    scores = jnp.where(allowed, scores, -1e30)
    attn_probs = jnp.exp(scores - row_lse[..., None])
    grad_values = jnp.einsum(
        "hqk,qhd->khd",
        attn_probs.astype(jnp.bfloat16),
        grad_context,
        preferred_element_type=jnp.float32,
    ).astype(jnp.bfloat16)
    grad_probs = jnp.einsum(
        "qhd,khd->hqk", grad_context, value_rows, preferred_element_type=jnp.float32
    )
    row_inner = jnp.sum(grad_probs * attn_probs, axis=-1, keepdims=True)
    grad_scores = (attn_probs * (grad_probs - row_inner)).astype(jnp.bfloat16)
    grad_queries = (
        jnp.einsum("hqk,khd->qhd", grad_scores, key_rows, preferred_element_type=jnp.float32)
        * scaling
    ).astype(jnp.bfloat16)
    grad_keys = (
        jnp.einsum("hqk,qhd->khd", grad_scores, queries, preferred_element_type=jnp.float32)
        * scaling
    ).astype(jnp.bfloat16)
    return jnp.stack([grad_queries, grad_keys, grad_values], axis=1)


def per_device(
    hidden_in,
    out_grad,
    ln1_gain,
    ln1_bias,
    w_query,
    w_key,
    w_value,
    w_out,
    ln2_gain,
    ln2_bias,
    w_up,
    b_up,
    w_down,
    b_down,
    rand_blocks,
):
    local_heads = rand_blocks.shape[0]
    head_width = local_heads * HD
    local_rows = hidden_in.shape[0]
    seq_count = local_rows * lax.axis_size("mp") // SEQ
    scaling = HD ** (-0.5)
    allowed = block_mask(rand_blocks)
    inputs = hidden_in.astype(jnp.float32)
    w_joined = jnp.concatenate([w_query, w_key, w_value], axis=1)
    normed_one = layer_norm(inputs, ln1_gain, ln1_bias).astype(jnp.bfloat16)
    rows_one = lax.all_gather(normed_one, "mp", axis=0, tiled=True)
    joined = jnp.dot(rows_one, w_joined, preferred_element_type=jnp.float32).astype(jnp.bfloat16)
    joined_seq = joined.reshape(seq_count, SEQ, 3, local_heads, HD)
    context, row_lse = lax.map(
        lambda seq_block: attend_forward(seq_block, allowed, scaling), joined_seq
    )
    context_rows = context.reshape(seq_count * SEQ, head_width)
    middle = inputs + lax.psum_scatter(
        jnp.dot(context_rows, w_out, preferred_element_type=jnp.float32).astype(jnp.bfloat16),
        "mp",
        scatter_dimension=0,
        tiled=True,
    ).astype(jnp.float32)
    normed_two = layer_norm(middle, ln2_gain, ln2_bias).astype(jnp.bfloat16)
    rows_two = lax.all_gather(normed_two, "mp", axis=0, tiled=True)
    up_pre = jnp.dot(rows_two, w_up, preferred_element_type=jnp.float32) + b_up
    hidden = jax.nn.gelu(up_pre, approximate=True).astype(jnp.bfloat16)
    output = (
        middle
        + (
            lax.psum_scatter(
                jnp.dot(hidden, w_down, preferred_element_type=jnp.float32).astype(jnp.bfloat16),
                "mp",
                scatter_dimension=0,
                tiled=True,
            ).astype(jnp.float32)
            + b_down
        )
    ).astype(jnp.bfloat16)
    grad_out = out_grad.astype(jnp.float32)
    bias_down = jnp.sum(grad_out, axis=0)
    rows_ffn = lax.all_gather(out_grad, "mp", axis=0, tiled=True)
    grad_hidden = jnp.einsum("nd,fd->nf", rows_ffn, w_down, preferred_element_type=jnp.float32)
    grad_down = jnp.einsum("nf,nd->fd", hidden, rows_ffn, preferred_element_type=jnp.float32)
    gelu_value, gelu_pull = jax.vjp(lambda pre_act: jax.nn.gelu(pre_act, approximate=True), up_pre)
    grad_up = gelu_pull(grad_hidden)[0].astype(jnp.bfloat16)
    bias_up = jnp.sum(grad_up, axis=0, dtype=jnp.float32)
    grad_up_weight = jnp.einsum("nd,nf->df", rows_two, grad_up, preferred_element_type=jnp.float32)
    grad_normed_two = lax.psum_scatter(
        jnp.einsum("nf,df->nd", grad_up, w_up, preferred_element_type=jnp.float32).astype(
            jnp.bfloat16
        ),
        "mp",
        scatter_dimension=0,
        tiled=True,
    ).astype(jnp.float32)
    norm_value_two, norm_pull_two = jax.vjp(layer_norm, middle, ln2_gain, ln2_bias)
    grad_mid_norm, gain_two, bias_two = norm_pull_two(grad_normed_two)
    grad_middle = grad_out + grad_mid_norm
    grad_attn = grad_middle.astype(jnp.bfloat16)
    rows_attn = lax.all_gather(grad_attn, "mp", axis=0, tiled=True)
    grad_context = jnp.einsum(
        "nd,ed->ne", rows_attn, w_out, preferred_element_type=jnp.float32
    ).astype(jnp.bfloat16)
    grad_out_weight = jnp.einsum(
        "ne,nd->ed", context_rows, rows_attn, preferred_element_type=jnp.float32
    )
    grad_joined = lax.map(
        lambda seq_items: attend_backward(seq_items, allowed, scaling),
        (joined_seq, grad_context.reshape(seq_count, SEQ, local_heads, HD), row_lse),
    )
    grad_joined = grad_joined.reshape(seq_count * SEQ, 3 * head_width)
    grad_joined_weight = jnp.einsum(
        "nd,ne->de", rows_one, grad_joined, preferred_element_type=jnp.float32
    )
    grad_normed_one = lax.psum_scatter(
        jnp.einsum("ne,de->nd", grad_joined, w_joined, preferred_element_type=jnp.float32).astype(
            jnp.bfloat16
        ),
        "mp",
        scatter_dimension=0,
        tiled=True,
    ).astype(jnp.float32)
    norm_value_one, norm_pull_one = jax.vjp(layer_norm, inputs, ln1_gain, ln1_bias)
    grad_in_norm, gain_one, bias_one = norm_pull_one(grad_normed_one)
    input_grad = grad_middle + grad_in_norm
    grad_joined_weight, grad_out_weight, grad_up_weight, bias_up, grad_down = (
        lax.psum(grad_joined_weight.astype(jnp.bfloat16), "dp").astype(jnp.float32),
        lax.psum(grad_out_weight.astype(jnp.bfloat16), "dp").astype(jnp.float32),
        lax.psum(grad_up_weight.astype(jnp.bfloat16), "dp").astype(jnp.float32),
        lax.psum(bias_up.astype(jnp.bfloat16), "dp").astype(jnp.float32),
        lax.psum(grad_down.astype(jnp.bfloat16), "dp").astype(jnp.float32),
    )
    gain_one, bias_one, gain_two, bias_two, bias_down = lax.psum(
        (gain_one, bias_one, gain_two, bias_two, bias_down), ("dp", "mp")
    )
    grad_query = grad_joined_weight[:, :head_width]
    grad_key = grad_joined_weight[:, head_width : 2 * head_width]
    grad_value = grad_joined_weight[:, 2 * head_width :]
    return (
        output,
        input_grad,
        gain_one,
        bias_one,
        grad_query,
        grad_key,
        grad_value,
        grad_out_weight,
        gain_two,
        bias_two,
        grad_up_weight,
        bias_up,
        grad_down,
        bias_down,
    )


def solution(mesh):
    in_specs = (
        P(("dp", "mp"), None),
        P(("dp", "mp"), None),
        P(),
        P(),
        P(None, "mp"),
        P(None, "mp"),
        P(None, "mp"),
        P("mp", None),
        P(),
        P(),
        P(None, "mp"),
        P("mp"),
        P("mp", None),
        P(),
        P("mp", None, None),
    )
    out_specs = (
        P(("dp", "mp"), None),
        P(("dp", "mp"), None),
        P(),
        P(),
        P(None, "mp"),
        P(None, "mp"),
        P(None, "mp"),
        P("mp", None),
        P(),
        P(),
        P(None, "mp"),
        P("mp"),
        P("mp", None),
        P(),
    )
    return jax.shard_map(
        per_device, mesh=mesh, in_specs=in_specs, out_specs=out_specs, check_vma=False
    )
```

profile of v0, /device:TPU:0, one launch (start us, length us, event | category | flops | bytes accessed | tf_op | source)
XLA Modules:
  0.0 1241.2 jit_solution(840713669255894146)
XLA Ops:
  22.0 52.6 %all-gather.5.cloned.1.call-done = bf16[2048,1024]{1,0:T(8,128)(2,1)} async-done(((bf16[1024,1024]{1,0:T(8,128)(2,1)}), bf16[2048,1024]{1,0:T(8,128)(2,1)}) %all-gather.5.cloned.1.call-update) | async-done | bytes 4194320 | tf_op jit(solution)/shard_map/all_gather | solution.py:107
  74.7 11.4 convolution_convert_fusion.2
  86.1 16.3 %reshape.244 = bf16[2,1024,3,8,64]{4,3,2,1,0:T(8,128)(2,1)} reshape(bf16[2048,1536]{1,0:T(8,128)(2,1)} %convolution_convert_fusion.2) | data formatting | bytes 12582912 | tf_op jit(solution)/shard_map/reshape | solution.py:109
  102.3 14.0 %copy.56 = bf16[2,1024,3,8,64]{1,4,3,2,0:T(8,128)(2,1)} copy(bf16[2,1024,3,8,64]{4,3,2,1,0:T(8,128)(2,1)} %reshape.244) | data formatting | bytes 12582912
  116.4 113.5 %while.24 = (s32[]{:T(128)}, bf16[2,1024,8,64]{1,3,2,0:T(8,128)(2,1)}, f32[2,8,1024]{2,1,0:T(8,128)S(1)}, bf16[2,1024,3,8,64]{1,4,3,2,0:T(8,128)(2,1)}, pred[8,1024,16]{1,2,0:T(8,128)(4,1)S(1)}, /*index=5*/s32[]{:T(128)}) while((s32[]{:T(128)}, bf16[2,1024,8,64]{1,3,2,0:T(8,128)(2,1)}, f32[2,8,1024]{2,1,0:T(8,128)S(1)}, ...), condition=%wide.region_6.7_spmd.clone, body=%wide.region_3.6_spmd.clone.sunk | while | flops 2248663040 | bytes 279576704 | solution.py:110
  118.7 13.2 %fusion.101 = (f32[8,1024]{1,0:T(8,128)S(1)}, f32[8,1024,1024]{1,2,0:T(8,128)}) fusion(pred[8,1024,16]{1,2,0:T(8,128)(4,1)S(1)} %get-tuple-element.292, bf16[1024,3,8,64]{0,3,2,1:T(8,128)(2,1)S(1)} %dynamic-slice_bitcast_fusion.6), kind=kOutput, calls=%fused_computation.5.clone.1 | convolution fusion | flops 1098899456 | bytes 35815424 | tf_op jit(solution)/shard_map/while/body/eval_jaxpr/qhd,khd->hqk/dot_general | solution.py:38
  131.9 14.7 %fusion.102 = f32[8,1024]{1,0:T(8,128)S(1)} fusion(f32[8,1024,1024]{1,2,0:T(8,128)} %get-tuple-element.264, f32[8,1024]{1,0:T(8,128)S(1)} %get-tuple-element.265, pred[8,1024,16]{1,2,0:T(8,128)(4,1)S(1)} %get-tuple-element.292), kind=kLoop, calls=%fused_computation.6.clone.1 | loop fusion | flops 33546240 | bytes 33751040 | tf_op jit(solution)/shard_map/while/body/eval_jaxpr/reduce_sum | solution.py:43
  152.2 10.9 divide_convert_fusion.2
  163.1 9.8 fusion.103
  175.3 13.2 %fusion.101 = (f32[8,1024]{1,0:T(8,128)S(1)}, f32[8,1024,1024]{1,2,0:T(8,128)}) fusion(pred[8,1024,16]{1,2,0:T(8,128)(4,1)S(1)} %get-tuple-element.292, bf16[1024,3,8,64]{0,3,2,1:T(8,128)(2,1)S(1)} %dynamic-slice_bitcast_fusion.6), kind=kOutput, calls=%fused_computation.5.clone.1 | convolution fusion | flops 1098899456 | bytes 35815424 | tf_op jit(solution)/shard_map/while/body/eval_jaxpr/qhd,khd->hqk/dot_general | solution.py:38
  188.4 14.7 %fusion.102 = f32[8,1024]{1,0:T(8,128)S(1)} fusion(f32[8,1024,1024]{1,2,0:T(8,128)} %get-tuple-element.264, f32[8,1024]{1,0:T(8,128)S(1)} %get-tuple-element.265, pred[8,1024,16]{1,2,0:T(8,128)(4,1)S(1)} %get-tuple-element.292), kind=kLoop, calls=%fused_computation.6.clone.1 | loop fusion | flops 33546240 | bytes 33751040 | tf_op jit(solution)/shard_map/while/body/eval_jaxpr/reduce_sum | solution.py:43
  208.7 10.9 divide_convert_fusion.2
  219.6 9.8 fusion.103
  240.1 54.4 %reduce-scatter.5.cloned.1.call-done = bf16[1024,1024]{1,0:T(8,128)(2,1)} async-done(((bf16[2048,1024]{1,0:T(8,128)(2,1)}), bf16[1024,1024]{1,0:T(8,128)(2,1)}) %reduce-scatter.5.cloned.1.call-update) | async-done | bytes 2097168 | tf_op jit(solution)/shard_map/reduce_scatter | solution.py:114
  300.9 56.3 %all-gather.7.cloned.1.call-done = bf16[2048,1024]{1,0:T(8,128)(2,1)} async-done(((bf16[1024,1024]{1,0:T(8,128)(2,1)}), bf16[2048,1024]{1,0:T(8,128)(2,1)}) %all-gather.7.cloned.1.call-update) | async-done | bytes 4194320 | tf_op jit(solution)/shard_map/all_gather | solution.py:121
  357.2 20.6 %multiply_convert_fusion.3 = (bf16[2048,2048]{1,0:T(8,128)(2,1)}, f32[2048,2048]{1,0:T(8,128)}) fusion(f32[2048]{0:T(1024)S(1)} %copy-done.44, bf16[2048,1024]{1,0:T(8,128)(2,1)} %all-gather.7.cloned.1.call-done, bf16[1024,2048]{1,0:T(8,128)(2,1)} %param.29), kind=kOutput, calls=%fused_computation.50 | convolution fusion | flops 8631877632 | bytes 33562624 | tf_op jit(solution)/shard_map/dot_general | solution.py:122
  377.8 37.6 %all-gather.9.cloned.1.call-done = bf16[2048,1024]{1,0:T(8,128)(2,1)} async-done(((bf16[1024,1024]{1,0:T(8,128)(2,1)}), bf16[2048,1024]{1,0:T(8,128)(2,1)}) %all-gather.9.cloned.1.call-update) | async-done | bytes 4194320 | tf_op jit(solution)/shard_map/all_gather | solution.py:138
  415.4 28.1 %fusion.55 = (bf16[2048]{0:T(1024)(128)(2,1)}, bf16[2048,2048]{1,0:T(8,128)(2,1)}) fusion(f32[2048,2048]{1,0:T(8,128)} %get-tuple-element.193, f32[2048]{0:T(1024)S(1)} %copy-done.44, bf16[2048,1024]{1,0:T(8,128)(2,1)} %all-gather.9.cloned.1.call-done, bf16[2048,1024]{1,0:T(8,128)(2,1)} %param.31), kind=kOutput, calls=%fused_computation.120 | convolution fusion | flops 8682207232 | bytes 33566720 | tf_op jit(solution)/shard_map/nd,fd->nf/dot_general | solution.py:139
  443.5 12.9 %convolution_convert_fusion.6 = bf16[2048,1024]{1,0:T(8,128)(2,1)} fusion(bf16[2048,2048]{1,0:T(8,128)(2,1)} %get-tuple-element.177, bf16[1024,2048]{1,0:T(8,128)(2,1)S(1)} %copy-done.41), kind=kOutput, calls=%fused_computation.87 | convolution fusion | flops 8592031744 | bytes 16777216 | tf_op jit(solution)/shard_map/nf,df->nd/dot_general | solution.py:146
  456.5 13.8 %convolution_convert_fusion.7 = bf16[2048,1024]{1,0:T(8,128)(2,1)} fusion(bf16[2048,2048]{1,0:T(8,128)(2,1)} %get-tuple-element.192, bf16[2048,1024]{1,0:T(8,128)(2,1)} %param.31), kind=kOutput, calls=%fused_computation.88 | convolution fusion | flops 8592031744 | bytes 16777216 | tf_op jit(solution)/shard_map/dot_general | solution.py:128
  470.4 40.5 %reduce-scatter.9.cloned.1.call-done = bf16[1024,1024]{1,0:T(8,128)(2,1)} async-done(((bf16[2048,1024]{1,0:T(8,128)(2,1)}), bf16[1024,1024]{1,0:T(8,128)(2,1)}) %reduce-scatter.9.cloned.1.call-update) | async-done | bytes 2097168 | tf_op jit(solution)/shard_map/reduce_scatter | solution.py:145
  515.3 52.0 %reduce-scatter.7.cloned.1.call-done = bf16[1024,1024]{1,0:T(8,128)(2,1)} async-done(((bf16[2048,1024]{1,0:T(8,128)(2,1)}), bf16[1024,1024]{1,0:T(8,128)(2,1)}) %reduce-scatter.7.cloned.1.call-update) | async-done | bytes 2097168 | tf_op jit(solution)/shard_map/reduce_scatter | solution.py:127
  567.4 5.5 fusion.57
  576.9 14.7 %convolution_convert_fusion.9 = bf16[2048,1024]{1,0:T(8,128)(2,1)} fusion(bf16[2048,2048]{1,0:T(8,128)(2,1)} %get-tuple-element.192, bf16[2048,1024]{1,0:T(8,128)(2,1)} %all-gather.9.cloned.1.call-done), kind=kOutput, calls=%fused_computation.90 | convolution fusion | flops 8592031744 | bytes 16777216 | tf_op jit(solution)/shard_map/nf,nd->fd/dot_general | solution.py:140
  591.6 13.1 %convolution_convert_fusion.5 = bf16[1024,2048]{1,0:T(8,128)(2,1)} fusion(bf16[2048,1024]{1,0:T(8,128)(2,1)S(1)} %copy-done.43, bf16[2048,2048]{1,0:T(8,128)(2,1)} %get-tuple-element.177), kind=kOutput, calls=%fused_computation.86 | convolution fusion | flops 8592031744 | bytes 16777216 | tf_op jit(solution)/shard_map/nd,nf->df/dot_general | solution.py:144
  604.7 29.0 %all-gather.11.cloned.1.call-done = bf16[2048,1024]{1,0:T(8,128)(2,1)} async-done(((bf16[1024,1024]{1,0:T(8,128)(2,1)}), bf16[2048,1024]{1,0:T(8,128)(2,1)}) %all-gather.11.cloned.1.call-update) | async-done | bytes 4194320 | tf_op jit(solution)/shard_map/all_gather | solution.py:157
  647.3 213.0 %while.25 = (s32[]{:T(128)}, bf16[2,1024,3,8,64]{1,4,3,2,0:T(8,128)(2,1)}, bf16[2,1024,3,8,64]{1,4,3,2,0:T(8,128)(2,1)}, f32[2,8,1024]{2,1,0:T(8,128)S(1)}, bf16...) while((s32[]{:T(128)}, ...), condition=%wide.region_16.17_spmd.clone, body=%wide.region_14.16_spmd.clone.sunk | while | flops 5481422848 | bytes 287768704 | solution.py:164
  649.7 13.1 %fusion.108 = f32[8,1024,1024]{1,2,0:T(8,128)} fusion(bf16[1024,3,8,64]{0,3,2,1:T(8,128)(2,1)S(1)} %dynamic-slice_bitcast_fusion.7), kind=kOutput, calls=%fused_computation.35.clone.1 | convolution fusion | flops 1073741824 | bytes 35651584 | tf_op jit(solution)/shard_map/while/body/eval_jaxpr/qhd,khd->hqk/dot_general | solution.py:55
  662.9 23.8 %multiply_reduce_fusion.3 = (f32[8,1024]{1,0:T(8,128)S(1)}, f32[8,1024,1024]{1,2,0:T(8,128)}) fusion(f32[8,1024,1024]{1,2,0:T(8,128)} %fusion.108, f32[8,1024]{1,0:T(8,128)S(1)} %dynamic-slice_bitcast_fusion.8, pred[8,1024,16]{1,2,0:T(8,128)(4,1)S(1)} %get-tuple-element.313, bf16[1024,3,8,64]{0,3,2,1:T(8,128)(2,1)S(1)} %dynamic-slice_bitcast_fusion.7, ...), kind=kOutput, calls=%fused_computation.17.clone.1 | convolution fusion | flops 1115676672 | bytes 69402624 | tf_op jit(solution)/shard_map/while/body/eval_jaxpr/qhd,khd->hqk/dot_general | solution.py:65
  686.7 33.3 %multiply_convert_fusion.5 = (bf16[8,1024,1024]{1,2,0:T(8,128)(2,1)}, bf16[8,1024,1024]{1,2,0:T(8,128)(2,1)}) fusion(f32[8,1024,1024]{1,2,0:T(8,128)} %get-tuple-element.272, f32[8,1024,1024]{1,2,0:T(8,128)} %fusion.108, f32[8,1024]{1,0:T(8,128)S(1)} %get-tuple-element.273, f32[8,1024]{1,0:T(8,128)S(1)} %dynamic-slice_bitcast_fusion.8, ...), kind=kLoop, calls=%fused_computation.16.clone.1 | loop fusion | flops 58720256 | bytes 100859904 | tf_op jit(solution)/shard_map/while/body/eval_jaxpr/convert_element_type | solution.py:69
  720.0 11.3 fusion.109
  731.3 9.1 fusion.111
  740.5 11.3 fusion.110
  756.1 13.1 %fusion.108 = f32[8,1024,1024]{1,2,0:T(8,128)} fusion(bf16[1024,3,8,64]{0,3,2,1:T(8,128)(2,1)S(1)} %dynamic-slice_bitcast_fusion.7), kind=kOutput, calls=%fused_computation.35.clone.1 | convolution fusion | flops 1073741824 | bytes 35651584 | tf_op jit(solution)/shard_map/while/body/eval_jaxpr/qhd,khd->hqk/dot_general | solution.py:55
  769.2 23.8 %multiply_reduce_fusion.3 = (f32[8,1024]{1,0:T(8,128)S(1)}, f32[8,1024,1024]{1,2,0:T(8,128)}) fusion(f32[8,1024,1024]{1,2,0:T(8,128)} %fusion.108, f32[8,1024]{1,0:T(8,128)S(1)} %dynamic-slice_bitcast_fusion.8, pred[8,1024,16]{1,2,0:T(8,128)(4,1)S(1)} %get-tuple-element.313, bf16[1024,3,8,64]{0,3,2,1:T(8,128)(2,1)S(1)} %dynamic-slice_bitcast_fusion.7, ...), kind=kOutput, calls=%fused_computation.17.clone.1 | convolution fusion | flops 1115676672 | bytes 69402624 | tf_op jit(solution)/shard_map/while/body/eval_jaxpr/qhd,khd->hqk/dot_general | solution.py:65
  793.1 33.3 %multiply_convert_fusion.5 = (bf16[8,1024,1024]{1,2,0:T(8,128)(2,1)}, bf16[8,1024,1024]{1,2,0:T(8,128)(2,1)}) fusion(f32[8,1024,1024]{1,2,0:T(8,128)} %get-tuple-element.272, f32[8,1024,1024]{1,2,0:T(8,128)} %fusion.108, f32[8,1024]{1,0:T(8,128)S(1)} %get-tuple-element.273, f32[8,1024]{1,0:T(8,128)S(1)} %dynamic-slice_bitcast_fusion.8, ...), kind=kLoop, calls=%fused_computation.16.clone.1 | loop fusion | flops 58720256 | bytes 100859904 | tf_op jit(solution)/shard_map/while/body/eval_jaxpr/convert_element_type | solution.py:69
  826.4 11.3 fusion.109
  837.7 9.1 fusion.111
  846.8 11.3 fusion.110
  860.4 11.9 copy.61
  875.0 7.8 convolution_convert_fusion.11
  882.8 8.2 convolution_convert_fusion.3
  891.1 11.9 convolution_convert_fusion.4
  903.7 35.2 %psum.77 = bf16[2048]{0:T(1024)(128)(2,1)S(1)} all-reduce(bf16[2048]{0:T(1024)(128)(2,1)S(1)} %copy-done.38), channel_id=1, replica_groups=mesh['dp'=16,'mp'=2] {'dp'}, use_global_device_ids=true, to_apply=%region_32.33 | all-reduce | flops 2048 | bytes 8192 | tf_op jit(solution)/shard_map/psum | solution.py:187
  939.5 186.7 %all-reduce.4.cloned.1.call-done = (bf16[1024,1536]{1,0:T(8,128)(2,1)}, bf16[512,1024]{1,0:T(8,128)(2,1)}, bf16[1024,2048]{1,0:T(8,128)(2,1)}, bf16[2048,1024]{1,0:T(8,128)(2,1)}) async-done(((bf16[1024,1536]{1,0:T(8,128)(2,1)}, bf16[512,1024]{1,0:T(8,128)(2,1)}, bf16[1024,2048]{1,0:T(8,128)(2,1)}, bf16[2048,1024]{1,0:T(8,128)(2,1)}), (bf16[1024,1536]{1,0:T(8,128)(2,1)}, bf16[512,1024]{1,0:T(8,128)(2,1)}, ...) | async-done | bytes 12582928 | tf_op jit(solution)/shard_map/psum | solution.py:184
  1129.0 6.9 convert_element_type.139
  1143.3 40.2 %reduce-scatter.11.cloned.1.call-done = bf16[1024,1024]{1,0:T(8,128)(2,1)} async-done(((bf16[2048,1024]{1,0:T(8,128)(2,1)}), bf16[1024,1024]{1,0:T(8,128)(2,1)}) %reduce-scatter.11.cloned.1.call-update) | async-done | bytes 2097168 | tf_op jit(solution)/shard_map/reduce_scatter | solution.py:172
  1194.4 39.8 %all-reduce = (f32[1024]{0:T(1024)}, f32[1024]{0:T(1024)}, f32[1024]{0:T(1024)}, f32[1024]{0:T(1024)}, f32[1024]{0:T(1024)}) all-reduce(f32[1024]{0:T(1024)S(1)} %get-tuple-element.140, f32[1024]{0:T(1024)S(1)} %get-tuple-element.143, f32[1024]{0:T(1024)S(1)} %copy-done.34, ...), channel_id=1, replica_groups=mesh['dp'=16,'mp'=2] {'dp','mp'}, use_global_device_ids=true, to_apply=%region_21.22 | all-reduce | flops 5120 | bytes 40960 | tf_op jit(solution)/shard_map/psum | solution.py:190
  (166 shorter events, 102.7 us)
Async XLA Ops:
  7.2 228.5 %copy-start = (bf16[512,1024]{1,0:T(8,128)(2,1)S(1)}, bf16[512,1024]{1,0:T(8,128)(2,1)}, u32[]{:S(2)}) copy-start(bf16[512,1024]{1,0:T(8,128)(2,1)} %param.26) | copy-start | bytes 3145732
  7.2 5.7 copy-start.4
  7.2 5.7 copy-start.27
  7.2 5.7 copy-start.39
  7.2 67.4 %all-gather.5.cloned.1.call-start = ((), (), s32[]{:S(2)}) async-start(), calls=%async_computation.4 | async-start | bytes 6291456 | tf_op jit(solution)/shard_map/all_gather | solution.py:107
  9.4 2.9 copy-start.23
  9.4 5.7 copy-start.36
  15.0 3.5 copy-start.20
  15.1 279.5 %reduce-scatter.5.cloned.1.call-start = ((), (), s32[]{:S(2)}) async-start(), calls=%async_computation.5 | async-start | bytes 6291456 | tf_op jit(solution)/shard_map/reduce_scatter | solution.py:114
  131.9 20.3 %copy-start.2 = (f32[8,1024,1024]{1,2,0:T(8,128)S(1)}, f32[8,1024,1024]{1,2,0:T(8,128)}, u32[]{:S(2)}) copy-start(f32[8,1024,1024]{1,2,0:T(8,128)} %get-tuple-element.264) | copy-start | bytes 100663296 | tf_op jit(solution)/shard_map/while
  188.4 20.3 %copy-start.2 = (f32[8,1024,1024]{1,2,0:T(8,128)S(1)}, f32[8,1024,1024]{1,2,0:T(8,128)}, u32[]{:S(2)}) copy-start(f32[8,1024,1024]{1,2,0:T(8,128)} %get-tuple-element.264) | copy-start | bytes 100663296 | tf_op jit(solution)/shard_map/while
  229.8 4.4 copy-start.7
  229.8 4.4 copy-start.21
  240.0 54.5 %copy-start.5 = (bf16[1024,1024]{1,0:T(8,128)(2,1)S(1)}, bf16[1024,1024]{1,0:T(8,128)(2,1)}, u32[]{:S(2)}) copy-start(bf16[1024,1024]{1,0:T(8,128)(2,1)} %param.19) | copy-start | bytes 6291460
  240.1 57.8 %copy-start.33 = (f32[1024]{0:T(1024)S(1)}, f32[1024]{0:T(1024)}, u32[]{:S(2)}) copy-start(f32[1024]{0:T(1024)} %param.27) | copy-start | bytes 12292
  240.1 57.8 %copy-start.37 = (f32[1024]{0:T(1024)S(1)}, f32[1024]{0:T(1024)}, u32[]{:S(2)}) copy-start(f32[1024]{0:T(1024)} %param.28) | copy-start | bytes 12292
  240.1 117.1 %all-gather.7.cloned.1.call-start = ((), (), s32[]{:S(2)}) async-start(), calls=%async_computation.6 | async-start | bytes 6291456 | tf_op jit(solution)/shard_map/all_gather | solution.py:121
  297.8 59.3 %copy-start.44 = (f32[2048]{0:T(1024)S(1)}, f32[2048]{0:T(1024)}, u32[]{:S(2)}) copy-start(f32[2048]{0:T(1024)} %param.30) | copy-start | bytes 24580
  300.2 115.2 %all-gather.9.cloned.1.call-start = ((), (), s32[]{:S(2)}) async-start(), calls=%async_computation.8 | async-start | bytes 6291456 | tf_op jit(solution)/shard_map/all_gather | solution.py:138
  300.8 210.1 %reduce-scatter.9.cloned.1.call-start = ((), (), s32[]{:S(2)}) async-start(), calls=%async_computation.9 | async-start | bytes 6291456 | tf_op jit(solution)/shard_map/reduce_scatter | solution.py:145
  415.4 28.1 %copy-start.41 = (bf16[1024,2048]{1,0:T(8,128)(2,1)S(1)}, bf16[1024,2048]{1,0:T(8,128)(2,1)}, u32[]{:S(2)}) copy-start(bf16[1024,2048]{1,0:T(8,128)(2,1)} %param.29) | copy-start | bytes 12582916
  456.4 110.9 %reduce-scatter.7.cloned.1.call-start = ((), (), s32[]{:S(2)}) async-start(), calls=%async_computation.7 | async-start | bytes 6291456 | tf_op jit(solution)/shard_map/reduce_scatter | solution.py:127
  470.3 97.0 %copy-start.40 = (f32[1024]{0:T(1024)S(1)}, f32[1024]{0:T(1024)}, u32[]{:S(2)}) copy-start(f32[1024]{0:T(1024)} %param.32) | copy-start | bytes 12292
  470.3 163.4 %all-gather.11.cloned.1.call-start = ((), (), s32[]{:S(2)}) async-start(), calls=%async_computation.10 | async-start | bytes 6291456 | tf_op jit(solution)/shard_map/all_gather | solution.py:157
  567.4 7.5 copy-start.13
  576.8 549.4 %all-reduce.4.cloned.1.call-start = ((), (), s32[]{:S(2)}) async-start(), calls=%async_computation.12 | async-start | bytes 25165824 | tf_op jit(solution)/shard_map/psum | solution.py:184
  576.9 14.7 %copy-start.43 = (bf16[2048,1024]{1,0:T(8,128)(2,1)S(1)}, bf16[2048,1024]{1,0:T(8,128)(2,1)}, u32[]{:S(2)}) copy-start(bf16[2048,1024]{1,0:T(8,128)(2,1)} %all-gather.7.cloned.1.call-done) | copy-start | bytes 12582916
  641.9 5.5 copy-start.8
  641.9 5.5 copy-start.22
  649.7 13.1 %copy-start.3 = (bf16[1024,3,8,64]{0,3,2,1:T(8,128)(2,1)}, bf16[1024,3,8,64]{0,3,2,1:T(8,128)(2,1)S(1)}, u32[]{:S(2)}) copy-start(bf16[1024,3,8,64]{0,3,2,1:T(8,128)(2,1)S(1)} %dynamic-slice_bitcast_fusion.7) | copy-start | bytes 9437188 | tf_op jit(solution)/shard_map/while
  756.1 13.2 %copy-start.3 = (bf16[1024,3,8,64]{0,3,2,1:T(8,128)(2,1)}, bf16[1024,3,8,64]{0,3,2,1:T(8,128)(2,1)S(1)}, u32[]{:S(2)}) copy-start(bf16[1024,3,8,64]{0,3,2,1:T(8,128)(2,1)S(1)} %dynamic-slice_bitcast_fusion.7) | copy-start | bytes 9437188 | tf_op jit(solution)/shard_map/while
  875.0 7.8 copy-start.16
  875.0 7.8 copy-start.42
  891.1 292.4 %reduce-scatter.11.cloned.1.call-start = ((), (), s32[]{:S(2)}) async-start(), calls=%async_computation.11 | async-start | bytes 6291456 | tf_op jit(solution)/shard_map/reduce_scatter | solution.py:172
  1129.0 6.9 copy-start.17
  1135.9 4.4 copy-start.15
  1140.3 43.2 %copy-start.6 = (bf16[1024,1024]{1,0:T(8,128)(2,1)S(1)}, bf16[1024,1024]{1,0:T(8,128)(2,1)}, u32[]{:S(2)}) copy-start(bf16[1024,1024]{1,0:T(8,128)(2,1)} %param.19) | copy-start | bytes 6291460
  1140.3 43.2 %copy-start.24 = (f32[1024]{0:T(1024)S(1)}, f32[1024]{0:T(1024)}, u32[]{:S(2)}) copy-start(f32[1024]{0:T(1024)} %copy-done.23) | copy-start | bytes 12292
  1140.3 43.2 %copy-start.28 = (f32[1024]{0:T(1024)S(1)}, f32[1024]{0:T(1024)}, u32[]{:S(2)}) copy-start(f32[1024]{0:T(1024)} %param.21) | copy-start | bytes 12292
  1143.3 43.3 %copy-start.32 = (f32[1024]{0:T(1024)S(1)}, f32[1024]{0:T(1024)}, u32[]{:S(2)}) copy-start(f32[1024]{0:T(1024)} %copy-done.31) | copy-start | bytes 12292
  1143.3 43.4 %copy-start.26 = (f32[1024]{0:T(1024)S(1)}, f32[1024]{0:T(1024)}, u32[]{:S(2)}) copy-start(f32[1024]{0:T(1024)} %copy-done.25) | copy-start | bytes 12292
  1143.3 47.3 %copy-start.30 = (f32[1024]{0:T(1024)S(1)}, f32[1024]{0:T(1024)}, u32[]{:S(2)}) copy-start(f32[1024]{0:T(1024)} %copy-done.29) | copy-start | bytes 12292
  1183.5 7.1 copy-start.11
  1183.5 7.1 copy-start.12
  1183.5 7.1 copy-start.14
  1190.6 43.6 %copy-start.1 = (bf16[512,1024]{1,0:T(8,128)(2,1)S(1)}, bf16[512,1024]{1,0:T(8,128)(2,1)}, u32[]{:S(2)}) copy-start(bf16[512,1024]{1,0:T(8,128)(2,1)} %param.26) | copy-start | bytes 3145732
  1190.6 3.7 copy-start.34
  1190.7 3.7 copy-start.35
  (8 other events, 12.2 us)
Sparse Core Ops, SparseCore 0:
  15.2 59.4 all-gather.4
  240.2 54.3 reduce-scatter.4
  300.4 56.7 all-gather.6
  358.6 56.7 all-gather.8
  456.5 54.3 reduce-scatter.8
  513.0 54.2 reduce-scatter.6
  576.9 56.7 all-gather.10
  891.2 234.9 all-reduce.3
  1129.1 54.3 reduce-scatter.10
where the time goes:
time: 1250 us; the launch traced here: 1240 us
  waiting for transfers between devices  550 us (44%)
  matrix products  335 us (27%)
  other arithmetic  172 us (14%)
  local copies, waits for them, and re-layouts  93.5 us (7%)
  blocking collectives  75.1 us (6%)
  between operations  14.8 us (1%)
    psum x1, waiting for transfers between devices, per_device(): lax.psum(grad_joined_weight.astype(jnp.bfloat16), 'dp').astype(jnp.float32)  187 us
    convert_element_type x2, other arithmetic, attend_backward(): grad_scores = (attn_probs * (grad_probs - row_inner)).astype(jnp.bfloat16)  66.6 us
    all_gather x1, waiting for transfers between devices, per_device(): rows_two = lax.all_gather(normed_two, 'mp', axis=0, tiled=True)  56.3 us
    reduce_scatter x1, waiting for transfers between devices, per_device(): lax.psum_scatter(jnp.dot(context_rows, w_out, preferred_element_type=jnp....  54.4 us
    all_gather x1, waiting for transfers between devices, per_device(): rows_one = lax.all_gather(normed_one, 'mp', axis=0, tiled=True)  52.6 us
    reduce_scatter x1, waiting for transfers between devices, per_device(): lax.psum_scatter(jnp.dot(hidden, w_down, preferred_element_type=jnp.float...  52 us
    dot_general x2, matrix products, attend_backward(): jnp.einsum('qhd,khd->hqk', grad_context, value_rows, preferred_element_ty...  47.7 us
    reduce_scatter x1, waiting for transfers between devices, per_device(): lax.psum_scatter(jnp.einsum('nf,df->nd', grad_up, w_up, preferred_element...  40.5 us
  transfers between devices with their start and end apart: 9, of which 9 were waited for; matrix products, arithmetic and copies ran while one was open for 8% of the time, Pallas kernels for 0%

commit v1 on v0

--- a/solution.py
+++ b/solution.py
@@ -188,7 +188,7 @@
         lax.psum(grad_down.astype(jnp.bfloat16), "dp").astype(jnp.float32),
     )
     gain_one, bias_one, gain_two, bias_two, bias_down = lax.psum(
-        (gain_one, bias_one, gain_two, bias_two, bias_down), ("dp", "mp")
+        lax.psum((gain_one, bias_one, gain_two, bias_two, bias_down), "mp"), "dp"
     )
     grad_query = grad_joined_weight[:, :head_width]
     grad_key = grad_joined_weight[:, head_width : 2 * head_width]

time: 1250 us -> 1270 us (1.016)
  blocking collectives: 75.1 us -> 102 us
    psum x1 -> x2, blocking collectives: 39.8 us -> 66.6 us  [the longest x1 59.5 us: per_device(): lax.psum(lax.psum((gain_one, bias_one, gain_two, bias_two, bias_down), 'm...]
where the time goes in v1:
time: 1270 us
  waiting for transfers between devices  550 us (43%)
  matrix products  335 us (26%)
  other arithmetic  172 us (14%)
  blocking collectives  102 us (8%)
  local copies, waits for them, and re-layouts  93.5 us (7%)
  between operations  14.8 us (1%)
    psum x1, waiting for transfers between devices, per_device(): lax.psum(grad_joined_weight.astype(jnp.bfloat16), 'dp').astype(jnp.float32)  187 us
    convert_element_type x2, other arithmetic, attend_backward(): grad_scores = (attn_probs * (grad_probs - row_inner)).astype(jnp.bfloat16)  66.6 us
    psum x1, blocking collectives, per_device(): lax.psum(lax.psum((gain_one, bias_one, gain_two, bias_two, bias_down), 'm...  59.5 us
    all_gather x1, waiting for transfers between devices, per_device(): rows_two = lax.all_gather(normed_two, 'mp', axis=0, tiled=True)  56.3 us
    reduce_scatter x1, waiting for transfers between devices, per_device(): lax.psum_scatter(jnp.dot(context_rows, w_out, preferred_element_type=jnp....  54.4 us
    all_gather x1, waiting for transfers between devices, per_device(): rows_one = lax.all_gather(normed_one, 'mp', axis=0, tiled=True)  52.7 us
    reduce_scatter x1, waiting for transfers between devices, per_device(): lax.psum_scatter(jnp.dot(hidden, w_down, preferred_element_type=jnp.float...  52 us
    dot_general x2, matrix products, attend_backward(): jnp.einsum('qhd,khd->hqk', grad_context, value_rows, preferred_element_ty...  47.6 us
  transfers between devices with their start and end apart: 9, of which 9 were waited for; matrix products, arithmetic and copies ran while one was open for 8% of the time, Pallas kernels for 0%

profile of v1, /device:TPU:0, one launch (start us, length us, event | category | flops | bytes accessed | tf_op | source)
XLA Modules:
  0.0 1267.8 jit_solution(14695005876477780070)
XLA Ops:
  22.0 52.7 %all-gather.5.cloned.1.call-done = bf16[2048,1024]{1,0:T(8,128)(2,1)} async-done(((bf16[1024,1024]{1,0:T(8,128)(2,1)}), bf16[2048,1024]{1,0:T(8,128)(2,1)}) %all-gather.5.cloned.1.call-update) | async-done | bytes 4194320 | tf_op jit(solution)/shard_map/all_gather | solution.py:107
  74.6 11.4 convolution_convert_fusion.2
  86.1 16.3 %reshape.244 = bf16[2,1024,3,8,64]{4,3,2,1,0:T(8,128)(2,1)} reshape(bf16[2048,1536]{1,0:T(8,128)(2,1)} %convolution_convert_fusion.2) | data formatting | bytes 12582912 | tf_op jit(solution)/shard_map/reshape | solution.py:109
  102.3 14.0 %copy.56 = bf16[2,1024,3,8,64]{1,4,3,2,0:T(8,128)(2,1)} copy(bf16[2,1024,3,8,64]{4,3,2,1,0:T(8,128)(2,1)} %reshape.244) | data formatting | bytes 12582912
  116.4 113.4 %while.24 = (s32[]{:T(128)}, bf16[2,1024,8,64]{1,3,2,0:T(8,128)(2,1)}, f32[2,8,1024]{2,1,0:T(8,128)S(1)}, bf16[2,1024,3,8,64]{1,4,3,2,0:T(8,128)(2,1)}, pred[8,1024,16]{1,2,0:T(8,128)(4,1)S(1)}, /*index=5*/s32[]{:T(128)}) while((s32[]{:T(128)}, bf16[2,1024,8,64]{1,3,2,0:T(8,128)(2,1)}, f32[2,8,1024]{2,1,0:T(8,128)S(1)}, ...), condition=%wide.region_6.7_spmd.clone, body=%wide.region_3.6_spmd.clone.sunk | while | flops 2248663040 | bytes 279576704 | solution.py:110
  118.7 13.1 %fusion.101 = (f32[8,1024]{1,0:T(8,128)S(1)}, f32[8,1024,1024]{1,2,0:T(8,128)}) fusion(pred[8,1024,16]{1,2,0:T(8,128)(4,1)S(1)} %get-tuple-element.297, bf16[1024,3,8,64]{0,3,2,1:T(8,128)(2,1)S(1)} %dynamic-slice_bitcast_fusion.6), kind=kOutput, calls=%fused_computation.5.clone.1 | convolution fusion | flops 1098899456 | bytes 35815424 | tf_op jit(solution)/shard_map/while/body/eval_jaxpr/qhd,khd->hqk/dot_general | solution.py:38
  131.9 14.7 %fusion.102 = f32[8,1024]{1,0:T(8,128)S(1)} fusion(f32[8,1024,1024]{1,2,0:T(8,128)} %get-tuple-element.269, f32[8,1024]{1,0:T(8,128)S(1)} %get-tuple-element.270, pred[8,1024,16]{1,2,0:T(8,128)(4,1)S(1)} %get-tuple-element.297), kind=kLoop, calls=%fused_computation.6.clone.1 | loop fusion | flops 33546240 | bytes 33751040 | tf_op jit(solution)/shard_map/while/body/eval_jaxpr/reduce_sum | solution.py:43
  152.2 10.9 divide_convert_fusion.2
  163.1 9.8 fusion.103
  175.3 13.1 %fusion.101 = (f32[8,1024]{1,0:T(8,128)S(1)}, f32[8,1024,1024]{1,2,0:T(8,128)}) fusion(pred[8,1024,16]{1,2,0:T(8,128)(4,1)S(1)} %get-tuple-element.297, bf16[1024,3,8,64]{0,3,2,1:T(8,128)(2,1)S(1)} %dynamic-slice_bitcast_fusion.6), kind=kOutput, calls=%fused_computation.5.clone.1 | convolution fusion | flops 1098899456 | bytes 35815424 | tf_op jit(solution)/shard_map/while/body/eval_jaxpr/qhd,khd->hqk/dot_general | solution.py:38
  188.4 14.7 %fusion.102 = f32[8,1024]{1,0:T(8,128)S(1)} fusion(f32[8,1024,1024]{1,2,0:T(8,128)} %get-tuple-element.269, f32[8,1024]{1,0:T(8,128)S(1)} %get-tuple-element.270, pred[8,1024,16]{1,2,0:T(8,128)(4,1)S(1)} %get-tuple-element.297), kind=kLoop, calls=%fused_computation.6.clone.1 | loop fusion | flops 33546240 | bytes 33751040 | tf_op jit(solution)/shard_map/while/body/eval_jaxpr/reduce_sum | solution.py:43
  208.7 10.9 divide_convert_fusion.2
  219.6 9.8 fusion.103
  240.1 54.4 %reduce-scatter.5.cloned.1.call-done = bf16[1024,1024]{1,0:T(8,128)(2,1)} async-done(((bf16[2048,1024]{1,0:T(8,128)(2,1)}), bf16[1024,1024]{1,0:T(8,128)(2,1)}) %reduce-scatter.5.cloned.1.call-update) | async-done | bytes 2097168 | tf_op jit(solution)/shard_map/reduce_scatter | solution.py:114
  300.8 56.3 %all-gather.7.cloned.1.call-done = bf16[2048,1024]{1,0:T(8,128)(2,1)} async-done(((bf16[1024,1024]{1,0:T(8,128)(2,1)}), bf16[2048,1024]{1,0:T(8,128)(2,1)}) %all-gather.7.cloned.1.call-update) | async-done | bytes 4194320 | tf_op jit(solution)/shard_map/all_gather | solution.py:121
  357.1 20.6 %multiply_convert_fusion.3 = (bf16[2048,2048]{1,0:T(8,128)(2,1)}, f32[2048,2048]{1,0:T(8,128)}) fusion(f32[2048]{0:T(1024)S(1)} %copy-done.44, bf16[2048,1024]{1,0:T(8,128)(2,1)} %all-gather.7.cloned.1.call-done, bf16[1024,2048]{1,0:T(8,128)(2,1)} %param.29), kind=kOutput, calls=%fused_computation.50 | convolution fusion | flops 8631877632 | bytes 33562624 | tf_op jit(solution)/shard_map/dot_general | solution.py:122
  377.7 37.6 %all-gather.9.cloned.1.call-done = bf16[2048,1024]{1,0:T(8,128)(2,1)} async-done(((bf16[1024,1024]{1,0:T(8,128)(2,1)}), bf16[2048,1024]{1,0:T(8,128)(2,1)}) %all-gather.9.cloned.1.call-update) | async-done | bytes 4194320 | tf_op jit(solution)/shard_map/all_gather | solution.py:138
  415.4 28.1 %fusion.55 = (bf16[2048]{0:T(1024)(128)(2,1)}, bf16[2048,2048]{1,0:T(8,128)(2,1)}) fusion(f32[2048,2048]{1,0:T(8,128)} %get-tuple-element.198, f32[2048]{0:T(1024)S(1)} %copy-done.44, bf16[2048,1024]{1,0:T(8,128)(2,1)} %all-gather.9.cloned.1.call-done, bf16[2048,1024]{1,0:T(8,128)(2,1)} %param.31), kind=kOutput, calls=%fused_computation.120 | convolution fusion | flops 8682207232 | bytes 33566720 | tf_op jit(solution)/shard_map/nd,fd->nf/dot_general | solution.py:139
  443.4 12.9 %convolution_convert_fusion.6 = bf16[2048,1024]{1,0:T(8,128)(2,1)} fusion(bf16[2048,2048]{1,0:T(8,128)(2,1)} %get-tuple-element.182, bf16[1024,2048]{1,0:T(8,128)(2,1)S(1)} %copy-done.41), kind=kOutput, calls=%fused_computation.87 | convolution fusion | flops 8592031744 | bytes 16777216 | tf_op jit(solution)/shard_map/nf,df->nd/dot_general | solution.py:146
  456.4 13.8 %convolution_convert_fusion.7 = bf16[2048,1024]{1,0:T(8,128)(2,1)} fusion(bf16[2048,2048]{1,0:T(8,128)(2,1)} %get-tuple-element.197, bf16[2048,1024]{1,0:T(8,128)(2,1)} %param.31), kind=kOutput, calls=%fused_computation.88 | convolution fusion | flops 8592031744 | bytes 16777216 | tf_op jit(solution)/shard_map/dot_general | solution.py:128
  470.3 40.5 %reduce-scatter.9.cloned.1.call-done = bf16[1024,1024]{1,0:T(8,128)(2,1)} async-done(((bf16[2048,1024]{1,0:T(8,128)(2,1)}), bf16[1024,1024]{1,0:T(8,128)(2,1)}) %reduce-scatter.9.cloned.1.call-update) | async-done | bytes 2097168 | tf_op jit(solution)/shard_map/reduce_scatter | solution.py:145
  515.3 52.0 %reduce-scatter.7.cloned.1.call-done = bf16[1024,1024]{1,0:T(8,128)(2,1)} async-done(((bf16[2048,1024]{1,0:T(8,128)(2,1)}), bf16[1024,1024]{1,0:T(8,128)(2,1)}) %reduce-scatter.7.cloned.1.call-update) | async-done | bytes 2097168 | tf_op jit(solution)/shard_map/reduce_scatter | solution.py:127
  576.8 14.7 %convolution_convert_fusion.9 = bf16[2048,1024]{1,0:T(8,128)(2,1)} fusion(bf16[2048,2048]{1,0:T(8,128)(2,1)} %get-tuple-element.197, bf16[2048,1024]{1,0:T(8,128)(2,1)} %all-gather.9.cloned.1.call-done), kind=kOutput, calls=%fused_computation.90 | convolution fusion | flops 8592031744 | bytes 16777216 | tf_op jit(solution)/shard_map/nf,nd->fd/dot_general | solution.py:140
  591.6 13.1 %convolution_convert_fusion.5 = bf16[1024,2048]{1,0:T(8,128)(2,1)} fusion(bf16[2048,1024]{1,0:T(8,128)(2,1)S(1)} %copy-done.43, bf16[2048,2048]{1,0:T(8,128)(2,1)} %get-tuple-element.182), kind=kOutput, calls=%fused_computation.86 | convolution fusion | flops 8592031744 | bytes 16777216 | tf_op jit(solution)/shard_map/nd,nf->df/dot_general | solution.py:144
  604.7 29.0 %all-gather.11.cloned.1.call-done = bf16[2048,1024]{1,0:T(8,128)(2,1)} async-done(((bf16[1024,1024]{1,0:T(8,128)(2,1)}), bf16[2048,1024]{1,0:T(8,128)(2,1)}) %all-gather.11.cloned.1.call-update) | async-done | bytes 4194320 | tf_op jit(solution)/shard_map/all_gather | solution.py:157
  647.3 212.9 %while.25 = (s32[]{:T(128)}, bf16[2,1024,3,8,64]{1,4,3,2,0:T(8,128)(2,1)}, bf16[2,1024,3,8,64]{1,4,3,2,0:T(8,128)(2,1)}, f32[2,8,1024]{2,1,0:T(8,128)S(1)}, bf16...) while((s32[]{:T(128)}, ...), condition=%wide.region_16.17_spmd.clone, body=%wide.region_14.16_spmd.clone.sunk | while | flops 5481422848 | bytes 287768704 | solution.py:164
  649.7 13.1 %fusion.108 = f32[8,1024,1024]{1,2,0:T(8,128)} fusion(bf16[1024,3,8,64]{0,3,2,1:T(8,128)(2,1)S(1)} %dynamic-slice_bitcast_fusion.7), kind=kOutput, calls=%fused_computation.35.clone.1 | convolution fusion | flops 1073741824 | bytes 35651584 | tf_op jit(solution)/shard_map/while/body/eval_jaxpr/qhd,khd->hqk/dot_general | solution.py:55
  662.9 23.8 %multiply_reduce_fusion.3 = (f32[8,1024]{1,0:T(8,128)S(1)}, f32[8,1024,1024]{1,2,0:T(8,128)}) fusion(f32[8,1024,1024]{1,2,0:T(8,128)} %fusion.108, f32[8,1024]{1,0:T(8,128)S(1)} %dynamic-slice_bitcast_fusion.8, pred[8,1024,16]{1,2,0:T(8,128)(4,1)S(1)} %get-tuple-element.318, bf16[1024,3,8,64]{0,3,2,1:T(8,128)(2,1)S(1)} %dynamic-slice_bitcast_fusion.7, ...), kind=kOutput, calls=%fused_computation.17.clone.1 | convolution fusion | flops 1115676672 | bytes 69402624 | tf_op jit(solution)/shard_map/while/body/eval_jaxpr/qhd,khd->hqk/dot_general | solution.py:65
  686.7 33.3 %multiply_convert_fusion.5 = (bf16[8,1024,1024]{1,2,0:T(8,128)(2,1)}, bf16[8,1024,1024]{1,2,0:T(8,128)(2,1)}) fusion(f32[8,1024,1024]{1,2,0:T(8,128)} %get-tuple-element.277, f32[8,1024,1024]{1,2,0:T(8,128)} %fusion.108, f32[8,1024]{1,0:T(8,128)S(1)} %get-tuple-element.278, f32[8,1024]{1,0:T(8,128)S(1)} %dynamic-slice_bitcast_fusion.8, ...), kind=kLoop, calls=%fused_computation.16.clone.1 | loop fusion | flops 58720256 | bytes 100859904 | tf_op jit(solution)/shard_map/while/body/eval_jaxpr/convert_element_type | solution.py:69
  720.0 11.3 fusion.109
  731.3 9.1 fusion.111
  740.4 11.3 fusion.110
  756.0 13.1 %fusion.108 = f32[8,1024,1024]{1,2,0:T(8,128)} fusion(bf16[1024,3,8,64]{0,3,2,1:T(8,128)(2,1)S(1)} %dynamic-slice_bitcast_fusion.7), kind=kOutput, calls=%fused_computation.35.clone.1 | convolution fusion | flops 1073741824 | bytes 35651584 | tf_op jit(solution)/shard_map/while/body/eval_jaxpr/qhd,khd->hqk/dot_general | solution.py:55
  769.1 23.8 %multiply_reduce_fusion.3 = (f32[8,1024]{1,0:T(8,128)S(1)}, f32[8,1024,1024]{1,2,0:T(8,128)}) fusion(f32[8,1024,1024]{1,2,0:T(8,128)} %fusion.108, f32[8,1024]{1,0:T(8,128)S(1)} %dynamic-slice_bitcast_fusion.8, pred[8,1024,16]{1,2,0:T(8,128)(4,1)S(1)} %get-tuple-element.318, bf16[1024,3,8,64]{0,3,2,1:T(8,128)(2,1)S(1)} %dynamic-slice_bitcast_fusion.7, ...), kind=kOutput, calls=%fused_computation.17.clone.1 | convolution fusion | flops 1115676672 | bytes 69402624 | tf_op jit(solution)/shard_map/while/body/eval_jaxpr/qhd,khd->hqk/dot_general | solution.py:65
  793.0 33.3 %multiply_convert_fusion.5 = (bf16[8,1024,1024]{1,2,0:T(8,128)(2,1)}, bf16[8,1024,1024]{1,2,0:T(8,128)(2,1)}) fusion(f32[8,1024,1024]{1,2,0:T(8,128)} %get-tuple-element.277, f32[8,1024,1024]{1,2,0:T(8,128)} %fusion.108, f32[8,1024]{1,0:T(8,128)S(1)} %get-tuple-element.278, f32[8,1024]{1,0:T(8,128)S(1)} %dynamic-slice_bitcast_fusion.8, ...), kind=kLoop, calls=%fused_computation.16.clone.1 | loop fusion | flops 58720256 | bytes 100859904 | tf_op jit(solution)/shard_map/while/body/eval_jaxpr/convert_element_type | solution.py:69
  826.2 11.3 fusion.109
  837.5 9.1 fusion.111
  846.7 11.3 fusion.110
  860.2 11.9 copy.61
  874.9 7.8 convolution_convert_fusion.11
  882.7 8.2 convolution_convert_fusion.3
  891.0 11.9 convolution_convert_fusion.4
  903.6 35.2 %psum.116 = bf16[2048]{0:T(1024)(128)(2,1)S(1)} all-reduce(bf16[2048]{0:T(1024)(128)(2,1)S(1)} %copy-done.38), channel_id=1, replica_groups=mesh['dp'=16,'mp'=2] {'dp'}, use_global_device_ids=true, to_apply=%region_36.37 | all-reduce | flops 2048 | bytes 8192 | tf_op jit(solution)/shard_map/psum | solution.py:187
  939.4 186.7 %all-reduce.5.cloned.1.call-done = (bf16[1024,1536]{1,0:T(8,128)(2,1)}, bf16[512,1024]{1,0:T(8,128)(2,1)}, bf16[1024,2048]{1,0:T(8,128)(2,1)}, bf16[2048,1024]{1,0:T(8,128)(2,1)}) async-done(((bf16[1024,1536]{1,0:T(8,128)(2,1)}, bf16[512,1024]{1,0:T(8,128)(2,1)}, bf16[1024,2048]{1,0:T(8,128)(2,1)}, bf16[2048,1024]{1,0:T(8,128)(2,1)}), (bf16[1024,1536]{1,0:T(8,128)(2,1)}, bf16[512,1024]{1,0:T(8,128)(2,1)}, ...) | async-done | bytes 12582928 | tf_op jit(solution)/shard_map/psum | solution.py:184
  1128.8 6.9 convert_element_type.139
  1143.2 40.2 %reduce-scatter.11.cloned.1.call-done = bf16[1024,1024]{1,0:T(8,128)(2,1)} async-done(((bf16[2048,1024]{1,0:T(8,128)(2,1)}), bf16[1024,1024]{1,0:T(8,128)(2,1)}) %reduce-scatter.11.cloned.1.call-update) | async-done | bytes 2097168 | tf_op jit(solution)/shard_map/reduce_scatter | solution.py:172
  1194.2 7.1 all-reduce.1
  1201.3 59.5 %all-reduce = (f32[1024]{0:T(1024)}, f32[1024]{0:T(1024)}, f32[1024]{0:T(1024)}, f32[1024]{0:T(1024)}, f32[1024]{0:T(1024)}) all-reduce(f32[1024]{0:T(1024)S(1)} %get-tuple-element.172, f32[1024]{0:T(1024)S(1)} %get-tuple-element.173, f32[1024]{0:T(1024)S(1)} %get-tuple-element.174, ...), channel_id=1, replica_groups=mesh['dp'=16,'mp'=2] {'dp'}, use_global_device_ids=true, to_apply=%region_22.23 | all-reduce | flops 5120 | bytes 40960 | tf_op jit(solution)/shard_map/psum | solution.py:190
  (167 shorter events, 108.2 us)
Async XLA Ops:
  7.2 228.4 %copy-start = (bf16[512,1024]{1,0:T(8,128)(2,1)S(1)}, bf16[512,1024]{1,0:T(8,128)(2,1)}, u32[]{:S(2)}) copy-start(bf16[512,1024]{1,0:T(8,128)(2,1)} %param.26) | copy-start | bytes 3145732
  7.2 5.7 copy-start.4
  7.2 5.7 copy-start.27
  7.2 5.7 copy-start.39
  7.2 67.4 %all-gather.5.cloned.1.call-start = ((), (), s32[]{:S(2)}) async-start(), calls=%async_computation.4 | async-start | bytes 6291456 | tf_op jit(solution)/shard_map/all_gather | solution.py:107
  9.4 2.9 copy-start.23
  9.4 5.7 copy-start.36
  15.0 3.6 copy-start.20
  15.1 279.4 %reduce-scatter.5.cloned.1.call-start = ((), (), s32[]{:S(2)}) async-start(), calls=%async_computation.5 | async-start | bytes 6291456 | tf_op jit(solution)/shard_map/reduce_scatter | solution.py:114
  131.9 20.3 %copy-start.2 = (f32[8,1024,1024]{1,2,0:T(8,128)S(1)}, f32[8,1024,1024]{1,2,0:T(8,128)}, u32[]{:S(2)}) copy-start(f32[8,1024,1024]{1,2,0:T(8,128)} %get-tuple-element.269) | copy-start | bytes 100663296 | tf_op jit(solution)/shard_map/while
  188.4 20.3 %copy-start.2 = (f32[8,1024,1024]{1,2,0:T(8,128)S(1)}, f32[8,1024,1024]{1,2,0:T(8,128)}, u32[]{:S(2)}) copy-start(f32[8,1024,1024]{1,2,0:T(8,128)} %get-tuple-element.269) | copy-start | bytes 100663296 | tf_op jit(solution)/shard_map/while
  229.8 4.4 copy-start.7
  229.8 4.4 copy-start.21
  240.0 54.5 %copy-start.5 = (bf16[1024,1024]{1,0:T(8,128)(2,1)S(1)}, bf16[1024,1024]{1,0:T(8,128)(2,1)}, u32[]{:S(2)}) copy-start(bf16[1024,1024]{1,0:T(8,128)(2,1)} %param.19) | copy-start | bytes 6291460
  240.0 57.7 %copy-start.33 = (f32[1024]{0:T(1024)S(1)}, f32[1024]{0:T(1024)}, u32[]{:S(2)}) copy-start(f32[1024]{0:T(1024)} %param.27) | copy-start | bytes 12292
  240.1 57.7 %copy-start.37 = (f32[1024]{0:T(1024)S(1)}, f32[1024]{0:T(1024)}, u32[]{:S(2)}) copy-start(f32[1024]{0:T(1024)} %param.28) | copy-start | bytes 12292
  240.1 117.0 %all-gather.7.cloned.1.call-start = ((), (), s32[]{:S(2)}) async-start(), calls=%async_computation.6 | async-start | bytes 6291456 | tf_op jit(solution)/shard_map/all_gather | solution.py:121
  297.8 59.3 %copy-start.44 = (f32[2048]{0:T(1024)S(1)}, f32[2048]{0:T(1024)}, u32[]{:S(2)}) copy-start(f32[2048]{0:T(1024)} %param.30) | copy-start | bytes 24580
  300.2 115.2 %all-gather.9.cloned.1.call-start = ((), (), s32[]{:S(2)}) async-start(), calls=%async_computation.8 | async-start | bytes 6291456 | tf_op jit(solution)/shard_map/all_gather | solution.py:138
  300.8 210.1 %reduce-scatter.9.cloned.1.call-start = ((), (), s32[]{:S(2)}) async-start(), calls=%async_computation.9 | async-start | bytes 6291456 | tf_op jit(solution)/shard_map/reduce_scatter | solution.py:145
  415.4 28.1 %copy-start.41 = (bf16[1024,2048]{1,0:T(8,128)(2,1)S(1)}, bf16[1024,2048]{1,0:T(8,128)(2,1)}, u32[]{:S(2)}) copy-start(bf16[1024,2048]{1,0:T(8,128)(2,1)} %param.29) | copy-start | bytes 12582916
  456.4 110.9 %reduce-scatter.7.cloned.1.call-start = ((), (), s32[]{:S(2)}) async-start(), calls=%async_computation.7 | async-start | bytes 6291456 | tf_op jit(solution)/shard_map/reduce_scatter | solution.py:127
  470.3 97.1 %copy-start.40 = (f32[1024]{0:T(1024)S(1)}, f32[1024]{0:T(1024)}, u32[]{:S(2)}) copy-start(f32[1024]{0:T(1024)} %param.32) | copy-start | bytes 12292
  470.3 163.4 %all-gather.11.cloned.1.call-start = ((), (), s32[]{:S(2)}) async-start(), calls=%async_computation.10 | async-start | bytes 6291456 | tf_op jit(solution)/shard_map/all_gather | solution.py:157
  567.3 7.5 copy-start.13
  576.8 549.3 %all-reduce.5.cloned.1.call-start = ((), (), s32[]{:S(2)}) async-start(), calls=%async_computation.12 | async-start | bytes 25165824 | tf_op jit(solution)/shard_map/psum | solution.py:184
  576.8 14.7 %copy-start.43 = (bf16[2048,1024]{1,0:T(8,128)(2,1)S(1)}, bf16[2048,1024]{1,0:T(8,128)(2,1)}, u32[]{:S(2)}) copy-start(bf16[2048,1024]{1,0:T(8,128)(2,1)} %all-gather.7.cloned.1.call-done) | copy-start | bytes 12582916
  641.8 5.5 copy-start.8
  641.8 5.5 copy-start.22
  649.7 13.1 %copy-start.3 = (bf16[1024,3,8,64]{0,3,2,1:T(8,128)(2,1)}, bf16[1024,3,8,64]{0,3,2,1:T(8,128)(2,1)S(1)}, u32[]{:S(2)}) copy-start(bf16[1024,3,8,64]{0,3,2,1:T(8,128)(2,1)S(1)} %dynamic-slice_bitcast_fusion.7) | copy-start | bytes 9437188 | tf_op jit(solution)/shard_map/while
  756.0 13.1 %copy-start.3 = (bf16[1024,3,8,64]{0,3,2,1:T(8,128)(2,1)}, bf16[1024,3,8,64]{0,3,2,1:T(8,128)(2,1)S(1)}, u32[]{:S(2)}) copy-start(bf16[1024,3,8,64]{0,3,2,1:T(8,128)(2,1)S(1)} %dynamic-slice_bitcast_fusion.7) | copy-start | bytes 9437188 | tf_op jit(solution)/shard_map/while
  874.9 7.8 copy-start.16
  874.9 7.8 copy-start.42
  890.9 292.4 %reduce-scatter.11.cloned.1.call-start = ((), (), s32[]{:S(2)}) async-start(), calls=%async_computation.11 | async-start | bytes 6291456 | tf_op jit(solution)/shard_map/reduce_scatter | solution.py:172
  1128.8 6.9 copy-start.17
  1135.7 4.4 copy-start.15
  1140.2 43.2 %copy-start.6 = (bf16[1024,1024]{1,0:T(8,128)(2,1)S(1)}, bf16[1024,1024]{1,0:T(8,128)(2,1)}, u32[]{:S(2)}) copy-start(bf16[1024,1024]{1,0:T(8,128)(2,1)} %param.19) | copy-start | bytes 6291460
  1140.2 43.2 %copy-start.24 = (f32[1024]{0:T(1024)S(1)}, f32[1024]{0:T(1024)}, u32[]{:S(2)}) copy-start(f32[1024]{0:T(1024)} %copy-done.23) | copy-start | bytes 12292
  1140.2 43.2 %copy-start.28 = (f32[1024]{0:T(1024)S(1)}, f32[1024]{0:T(1024)}, u32[]{:S(2)}) copy-start(f32[1024]{0:T(1024)} %param.21) | copy-start | bytes 12292
  1143.2 43.3 %copy-start.32 = (f32[1024]{0:T(1024)S(1)}, f32[1024]{0:T(1024)}, u32[]{:S(2)}) copy-start(f32[1024]{0:T(1024)} %copy-done.31) | copy-start | bytes 12292
  1143.2 43.4 %copy-start.26 = (f32[1024]{0:T(1024)S(1)}, f32[1024]{0:T(1024)}, u32[]{:S(2)}) copy-start(f32[1024]{0:T(1024)} %copy-done.25) | copy-start | bytes 12292
  1143.2 47.3 %copy-start.30 = (f32[1024]{0:T(1024)S(1)}, f32[1024]{0:T(1024)}, u32[]{:S(2)}) copy-start(f32[1024]{0:T(1024)} %copy-done.29) | copy-start | bytes 12292
  1183.4 7.1 copy-start.11
  1183.4 7.1 copy-start.12
  1183.4 7.1 copy-start.14
  1190.4 70.4 %copy-start.1 = (bf16[512,1024]{1,0:T(8,128)(2,1)S(1)}, bf16[512,1024]{1,0:T(8,128)(2,1)}, u32[]{:S(2)}) copy-start(bf16[512,1024]{1,0:T(8,128)(2,1)} %param.26) | copy-start | bytes 3145732
  1190.5 3.7 copy-start.34
  1190.5 3.7 copy-start.35
  (8 other events, 12.2 us)
Sparse Core Ops, SparseCore 0:
  15.2 59.4 all-gather.4
  240.2 54.2 reduce-scatter.4
  300.3 56.7 all-gather.6
  358.6 56.7 all-gather.8
  456.5 54.3 reduce-scatter.8
  513.0 54.2 reduce-scatter.6
  576.9 56.7 all-gather.10
  891.1 234.9 all-reduce.4
  1129.0 54.3 reduce-scatter.10
